TPU v7x, 512 devices: a whole 4x4x16 slice. The times are simulated.
512 devices in a mesh: tm: 64 (over y, z), head: 8 (over x, core).
Axes of the slice: x: 4, y: 4, z: 16, core: 2. Of those that a mesh axis runs over, the one named last changes fastest.
Arguments:
- queries: bfloat16 [16384, 3072], P('tm', 'head'), may hold values from -170 to 170
- key_rows: bfloat16 [16384, 3072], P('tm', 'head'), may hold values from -6 to 6
- value_rows: bfloat16 [16384, 3072], P('tm', 'head'), may hold values from -102 to 102
- grad_normed: bfloat16 [16384, 3072], P('tm', 'head'), may hold values from -5.5 to 5.5
- norm_gain: float32 [3072], P('head'), may hold values from 0.25 to 1.75
- utter_ids: int32 [128], P('tm'), may hold values from 0 to 20, never falling along the last dimension, each value on 1 to 8 neighbouring positions
Outputs:
- normed: bfloat16 [16384, 3072], P('tm', 'head')
- grad_queries: bfloat16 [16384, 3072], P('tm', 'head')
- grad_keys: bfloat16 [16384, 3072], P('tm', 'head')
- grad_values: bfloat16 [16384, 3072], P('tm', 'head')
- grad_gain: float32 [3072], P('head')
Inputs may be any that keep to these rules, and one draw needn't show every extreme that they name: `utter_ids`: ids never fall; each utterance covers 1 to 8 consecutive blocks of 128 frames, and one covers exactly 8.
All inputs are finite; a program needn't handle non-finite values.
Results may differ from a plain program's by a relative error of at most 0.024.
Values may be sent and summed in bfloat16 or wider, within the bound.
A program may use at most 64 MiB of HBM per device.

v0:
```python
import jax
import jax.numpy as jnp
from jax import lax
from jax.sharding import PartitionSpec as P

HSZ = 128
REACH = 4


def for_sending(x):

    def short(part):
        return part.astype(jnp.bfloat16) if part.dtype == jnp.float32 else part

    return jax.tree.map(short, x)


def passed_along(x, axis, by):
    length = lax.axis_size(axis)
    pairs = [(i, i + by) for i in range(length) if 0 <= i + by < length]
    return lax.ppermute(x, axis, pairs)


def frame_utter(utter_ids, row_count):
    blocks = utter_ids.shape[0]
    spread = jnp.broadcast_to(utter_ids[:, None] + 1, (blocks, row_count // blocks))
    return spread.reshape(row_count)


def rounded_term(term):
    return lax.optimization_barrier(term.astype(jnp.bfloat16)).astype(jnp.float32)


def tile_scores(query_heads, key_heads, query_utt, key_utt, factor):
    scores = (
        jnp.einsum("qhe,khe->hqk", query_heads, key_heads, preferred_element_type=jnp.float32)
        * factor
    )
    allowed = query_utt[:, None] == key_utt[None, :]
    return jnp.where(allowed[None], scores, -jnp.inf)


def lse_step(query_heads, query_utt, key_heads, key_utt, factor, current):
    top_score, exp_total = current
    scores = tile_scores(query_heads, key_heads, query_utt, key_utt, factor)
    new_top = jnp.maximum(top_score, jnp.max(scores, axis=2))
    exp_total = exp_total * jnp.exp(top_score - new_top) + jnp.sum(
        jnp.exp(scores - new_top[:, :, None]), axis=2
    )
    return (new_top, exp_total)


def output_step(
    query_heads, query_utt, key_heads, value_heads, key_utt, log_total, factor, out_accum
):
    weights = jnp.exp(
        tile_scores(query_heads, key_heads, query_utt, key_utt, factor) - log_total[:, :, None]
    )
    return out_accum + jnp.einsum(
        "hqk,khe->qhe",
        weights.astype(jnp.bfloat16),
        value_heads,
        preferred_element_type=jnp.float32,
    )


def tile_grads(
    query_heads,
    grad_heads,
    key_heads,
    value_heads,
    query_utt,
    key_utt,
    log_total,
    row_delta,
    factor,
):
    scores = tile_scores(query_heads, key_heads, query_utt, key_utt, factor)
    weights = jnp.exp(scores - log_total[:, :, None])
    grad_weights = jnp.einsum(
        "qhe,khe->hqk", grad_heads, value_heads, preferred_element_type=jnp.float32
    )
    dscore = (weights * (grad_weights - row_delta[:, :, None])).astype(jnp.bfloat16)
    return (weights.astype(jnp.bfloat16), dscore)


def query_step(
    query_heads,
    grad_heads,
    key_heads,
    value_heads,
    query_utt,
    key_utt,
    log_total,
    row_delta,
    factor,
    current,
):
    weights_b, dscore = tile_grads(
        query_heads,
        grad_heads,
        key_heads,
        value_heads,
        query_utt,
        key_utt,
        log_total,
        row_delta,
        factor,
    )
    grad_query = (
        current[0]
        + jnp.einsum("hqk,khe->qhe", dscore, key_heads, preferred_element_type=jnp.float32) * factor
    )
    key_grad = (
        jnp.einsum("hqk,qhe->khe", dscore, query_heads, preferred_element_type=jnp.float32) * factor
    )
    value_grad = jnp.einsum(
        "hqk,qhe->khe", weights_b, grad_heads, preferred_element_type=jnp.float32
    )
    return (grad_query, key_grad, value_grad)


def body(queries, key_rows, value_rows, grad_normed, norm_gain, utter_ids):
    row_count, feat_width = queries.shape
    head_count = feat_width // HSZ
    factor = HSZ ** (-0.5)
    layout = (row_count, head_count, HSZ)
    query_heads = queries.reshape(layout)
    own_utt = frame_utter(utter_ids, row_count)
    own_pair = jnp.stack([key_rows, value_rows])
    sources = [(own_pair, own_utt)]
    moving = (own_pair, own_utt)
    for distance in range(REACH):
        moving = passed_along((moving[0], for_sending(moving[1])), "tm", 1)
        sources.append(moving)
    key_blocks = []
    for source in sources:
        pair_rows = source[0]
        key_utt = source[1]
        live = jnp.any(own_utt[:, None] == key_utt[None, :])
        key_blocks.append(
            (pair_rows[0].reshape(layout), pair_rows[1].reshape(layout), key_utt, live)
        )
    top_score = jnp.full((head_count, row_count), -jnp.inf, jnp.float32)
    exp_total = jnp.zeros((head_count, row_count), jnp.float32)
    for key_block in key_blocks:
        top_score, exp_total = lse_step(
            query_heads, own_utt, key_block[0], key_block[2], factor, (top_score, exp_total)
        )
    log_total = top_score + jnp.log(exp_total)
    out_accum = jnp.zeros(layout, jnp.float32)
    for key_block in key_blocks:
        out_accum = output_step(
            query_heads,
            own_utt,
            key_block[0],
            key_block[1],
            key_block[2],
            log_total,
            factor,
            out_accum,
        )
    attended = out_accum.astype(jnp.bfloat16)
    flat_att = attended.reshape(row_count, feat_width).astype(jnp.float32)
    features = feat_width * lax.axis_size("head")
    grad_rows = grad_normed.astype(jnp.float32)
    scaled = grad_rows * norm_gain
    square_sum, cross_sum = lax.psum(
        (jnp.sum(flat_att * flat_att, axis=1), jnp.sum(scaled * flat_att, axis=1)), "head"
    )
    rms_inv = 1.0 / jnp.sqrt(square_sum / features + 1e-06)
    normed = (flat_att * rms_inv[:, None] * norm_gain).astype(jnp.bfloat16)
    grad_att = (
        rms_inv[:, None] * (scaled - flat_att * (rms_inv * rms_inv * cross_sum / features)[:, None])
    ).astype(jnp.bfloat16)
    grad_gain = lax.psum(jnp.sum(grad_rows * flat_att * rms_inv[:, None], axis=0), "tm")
    grad_heads = grad_att.reshape(layout)
    row_delta = jnp.sum(attended.astype(jnp.float32) * grad_heads.astype(jnp.float32), axis=2).T
    zero_heads = jnp.zeros(layout, jnp.float32)
    grad_query = zero_heads
    key_parts = []
    for key_block in key_blocks:
        grad_query, key_grad, value_grad = query_step(
            query_heads,
            grad_heads,
            key_block[0],
            key_block[1],
            own_utt,
            key_block[2],
            log_total,
            row_delta,
            factor,
            (grad_query, zero_heads, zero_heads),
        )
        key_parts.append(
            jnp.stack(
                [key_grad.reshape(row_count, feat_width), value_grad.reshape(row_count, feat_width)]
            )
        )
    carried = rounded_term(key_parts[0])
    for distance in range(1, REACH + 1):
        arrived = passed_along(key_parts[distance].astype(jnp.bfloat16), "tm", -distance)
        carried = carried + arrived.astype(jnp.float32)
    grad_queries = grad_query.reshape(row_count, feat_width).astype(jnp.bfloat16)
    return (
        normed,
        grad_queries,
        carried[0].astype(jnp.bfloat16),
        carried[1].astype(jnp.bfloat16),
        grad_gain,
    )


def solution(mesh):
    in_specs = (
        P("tm", "head"),
        P("tm", "head"),
        P("tm", "head"),
        P("tm", "head"),
        P("head"),
        P("tm"),
    )
    out_specs = (P("tm", "head"), P("tm", "head"), P("tm", "head"), P("tm", "head"), P("head"))
    return jax.shard_map(body, mesh=mesh, in_specs=in_specs, out_specs=out_specs, check_vma=False)
```

profile of v0, /device:TPU:6, one launch (start us, length us, event | category | flops | bytes accessed | tf_op | source)
XLA Modules:
  0.0 350.9 jit_solution(14660419836064884476)
XLA Ops:
  0.6 0.7 broadcast_add_fusion
  1.4 3.9 %collective-permute-start = (s32[256]{0:T(256)S(1)}, s32[256]{0:T(256)S(1)}, u32[]{:S(2)}, u32[]{:S(2)}) collective-permute-start(s32[256]{0:T(256)S(1)} %broadcast_bitcast_fusion), channel_id=1, source_target_pairs={{0,8},{8,16},{16,24},{24,32},{32,40},{40,48},{48,56},{56,64},{64,7... | collective-permute-start | bytes 3080 | tf_op jit(solution)/shard_map/ppermute | solution.py:21
  5.3 1.3 collective-permute-done
  6.6 4.2 %collective-permute-start.2 = (s32[256]{0:T(256)S(1)}, s32[256]{0:T(256)S(1)}, u32[]{:S(2)}, u32[]{:S(2)}) collective-permute-start(s32[256]{0:T(256)S(1)} %collective-permute-done), channel_id=1, source_target_pairs={{0,8},{8,16},{16,24},{24,32},{32,40},{40,48},{48,56},{56,64},{64,7... | collective-permute-start | bytes 3080 | tf_op jit(solution)/shard_map/ppermute | solution.py:21
  10.8 1.3 collective-permute-done.2
  12.0 4.2 %collective-permute-start.4 = (s32[256]{0:T(256)S(1)}, s32[256]{0:T(256)S(1)}, u32[]{:S(2)}, u32[]{:S(2)}) collective-permute-start(s32[256]{0:T(256)S(1)} %collective-permute-done.2), channel_id=1, source_target_pairs={{0,8},{8,16},{16,24},{24,32},{32,40},{40,48},{48,56},{56,64},{64,7... | collective-permute-start | bytes 3080 | tf_op jit(solution)/shard_map/ppermute | solution.py:21
  16.2 1.1 copy.85
  17.5 4.3 %collective-permute-start.6 = (s32[256]{0:T(256)S(1)}, s32[256]{0:T(256)S(1)}, u32[]{:S(2)}, u32[]{:S(2)}) collective-permute-start(s32[256]{0:T(256)S(1)} %collective-permute-done.4), channel_id=1, source_target_pairs={{0,8},{8,16},{16,24},{24,32},{32,40},{40,48},{48,56},{56,64},{64,7... | collective-permute-start | bytes 3080 | tf_op jit(solution)/shard_map/ppermute | solution.py:21
  21.9 5.5 %collective-permute-start.1 = (bf16[2,256,384]{1,2,0:T(8,128)(2,1)S(1)}, bf16[2,256,384]{1,2,0:T(8,128)(2,1)S(1)}, u32[]{:S(2)}, u32[]{:S(2)}) collective-permute-start(bf16[2,256,384]{1,2,0:T(8,128)(2,1)S(1)} %pad_maximum_fusion), channel_id=1, source_target_pairs={{0,8},{8,16},{16,24},{24,32},{32,40},{40,48},{48,56},{56,64},{64,7... | collective-permute-start | bytes 1179656 | tf_op jit(solution)/shard_map/ppermute | solution.py:21
  28.4 4.8 %collective-permute-done.1 = bf16[2,256,384]{1,2,0:T(8,128)(2,1)S(1)} collective-permute-done((bf16[2,256,384]{1,2,0:T(8,128)(2,1)S(1)}, bf16[2,256,384]{1,2,0:T(8,128)(2,1)S(1)}, u32[]{:S(2)}, u32[]{:S(2)}) %collective-permute-start.1) | collective-permute-done | bytes 393248 | tf_op jit(solution)/shard_map/ppermute | solution.py:21
  33.2 5.1 %collective-permute-start.3 = (bf16[2,256,384]{1,2,0:T(8,128)(2,1)S(1)}, bf16[2,256,384]{1,2,0:T(8,128)(2,1)S(1)}, u32[]{:S(2)}, u32[]{:S(2)}) collective-permute-start(bf16[2,256,384]{1,2,0:T(8,128)(2,1)S(1)} %collective-permute-done.1), channel_id=1, source_target_pairs={{0,8},{8,16},{16,24},{24,32},{32,40},{40,48},{48,56},{56,64},{64,7... | collective-permute-start | bytes 1179656 | tf_op jit(solution)/shard_map/ppermute | solution.py:21
  39.0 4.8 %collective-permute-done.3 = bf16[2,256,384]{1,2,0:T(8,128)(2,1)S(1)} collective-permute-done((bf16[2,256,384]{1,2,0:T(8,128)(2,1)S(1)}, bf16[2,256,384]{1,2,0:T(8,128)(2,1)S(1)}, u32[]{:S(2)}, u32[]{:S(2)}) %collective-permute-start.3) | collective-permute-done | bytes 393248 | tf_op jit(solution)/shard_map/ppermute | solution.py:21
  43.8 6.7 %collective-permute-start.5 = (bf16[2,256,384]{1,2,0:T(8,128)(2,1)S(1)}, bf16[2,256,384]{1,2,0:T(8,128)(2,1)S(1)}, u32[]{:S(2)}, u32[]{:S(2)}) collective-permute-start(bf16[2,256,384]{1,2,0:T(8,128)(2,1)S(1)} %collective-permute-done.3), channel_id=1, source_target_pairs={{0,8},{8,16},{16,24},{24,32},{32,40},{40,48},{48,56},{56,64},{64,7... | collective-permute-start | bytes 1179656 | tf_op jit(solution)/shard_map/ppermute | solution.py:21
  51.2 6.6 %collective-permute-done.5 = bf16[2,256,384]{1,2,0:T(8,128)(2,1)S(1)} collective-permute-done((bf16[2,256,384]{1,2,0:T(8,128)(2,1)S(1)}, bf16[2,256,384]{1,2,0:T(8,128)(2,1)S(1)}, u32[]{:S(2)}, u32[]{:S(2)}) %collective-permute-start.5) | collective-permute-done | bytes 393248 | tf_op jit(solution)/shard_map/ppermute | solution.py:21
  57.9 5.0 %collective-permute-start.7 = (bf16[2,256,384]{1,2,0:T(8,128)(2,1)S(1)}, bf16[2,256,384]{1,2,0:T(8,128)(2,1)S(1)}, u32[]{:S(2)}, u32[]{:S(2)}) collective-permute-start(bf16[2,256,384]{1,2,0:T(8,128)(2,1)S(1)} %collective-permute-done.5), channel_id=1, source_target_pairs={{0,8},{8,16},{16,24},{24,32},{32,40},{40,48},{48,56},{56,64},{64,7... | collective-permute-start | bytes 1179656 | tf_op jit(solution)/shard_map/ppermute | solution.py:21
  63.6 4.5 %collective-permute-done.7 = bf16[2,256,384]{1,2,0:T(8,128)(2,1)S(1)} collective-permute-done((bf16[2,256,384]{1,2,0:T(8,128)(2,1)S(1)}, bf16[2,256,384]{1,2,0:T(8,128)(2,1)S(1)}, u32[]{:S(2)}, u32[]{:S(2)}) %collective-permute-start.7) | collective-permute-done | bytes 393248 | tf_op jit(solution)/shard_map/ppermute | solution.py:21
  70.8 1.1 multiply_reduce_fusion.1
  71.8 10.0 %psum.21 = f32[256]{0:T(256)S(1)} all-reduce(f32[256]{0:T(256)S(1)} %get-tuple-element.48), channel_id=1, replica_groups=mesh['tm'=64,'head'=8] {'head'}, use_global_device_ids=true, to_apply=%region_11.12 | all-reduce | flops 256 | bytes 2048 | tf_op jit(solution)/shard_map/psum | solution.py:168
  81.8 2.0 copy.105
  83.8 1.7 fusion.47
  85.5 12.0 %psum.22 = f32[256]{0:T(256)} all-reduce(f32[256]{0:T(256)} %get-tuple-element.16), channel_id=1, replica_groups=mesh['tm'=64,'head'=8] {'head'}, use_global_device_ids=true, to_apply=%region_13.14 | all-reduce | flops 256 | bytes 2048 | tf_op jit(solution)/shard_map/psum | solution.py:168
  97.6 0.7 multiply_multiply_fusion
  98.3 1.9 fusion.45
  100.2 1.1 copy.108
  101.2 1.1 multiply_reduce_fusion
  102.3 1.0 convolution_convert_fusion.3
  103.4 1.1 fusion.11
  104.5 1.1 fusion.12
  105.6 1.0 convolution_convert_fusion.2
  107.0 1.0 convolution_convert_fusion.1
  110.8 0.8 copy-done.33
  111.8 0.8 copy-done.34
  112.9 0.8 copy-done.5
  113.8 0.8 copy-done.3
  115.8 0.8 copy-done.2
  117.7 1.0 fusion.32
  120.5 0.8 pad_maximum_fusion.2
  121.3 1.3 collective-permute-start.8
  122.6 0.8 pad_maximum_fusion.3
  123.4 1.3 collective-permute-start.9
  124.7 0.8 pad_maximum_fusion.5
  125.5 1.4 collective-permute-start.11
  126.9 0.8 pad_maximum_fusion.4
  127.7 1.3 collective-permute-start.10
  129.4 0.8 copy.150
  131.4 217.4 %psum.23 = f32[384]{0:T(512)} all-reduce(f32[384]{0:T(512)S(1)} %copy-done.40), channel_id=1, replica_groups=mesh['tm'=64,'head'=8] {'tm'}, use_global_device_ids=true, to_apply=%region_16.17 | all-reduce | flops 384 | bytes 3072 | tf_op jit(solution)/shard_map/psum | solution.py:176
  348.8 1.2 add_convert_fusion
  350.1 0.8 slice_bitcast_fusion
  (132 shorter events, 15.2 us)
Async XLA Ops:
  1.4 15.9 %copy-start.37 = (bf16[256,384]{1,0:T(8,128)(2,1)S(1)}, bf16[256,384]{1,0:T(8,128)(2,1)}, u32[]{:S(2)}) copy-start(bf16[256,384]{1,0:T(8,128)(2,1)} %param.8) | copy-start | bytes 589828
  1.4 5.2 %collective-permute-start = (s32[256]{0:T(256)S(1)}, s32[256]{0:T(256)S(1)}, u32[]{:S(2)}, u32[]{:S(2)}) collective-permute-start(s32[256]{0:T(256)S(1)} %broadcast_bitcast_fusion), channel_id=1, source_target_pairs={{0,8},{8,16},{16,24},{24,32},{32,40},{40,48},{48,56},{56,64},{64,7... | collective-permute-start | bytes 3080 | tf_op jit(solution)/shard_map/ppermute | solution.py:21
  6.6 5.5 %collective-permute-start.2 = (s32[256]{0:T(256)S(1)}, s32[256]{0:T(256)S(1)}, u32[]{:S(2)}, u32[]{:S(2)}) collective-permute-start(s32[256]{0:T(256)S(1)} %collective-permute-done), channel_id=1, source_target_pairs={{0,8},{8,16},{16,24},{24,32},{32,40},{40,48},{48,56},{56,64},{64,7... | collective-permute-start | bytes 3080 | tf_op jit(solution)/shard_map/ppermute | solution.py:21
  12.0 5.5 %collective-permute-start.4 = (s32[256]{0:T(256)S(1)}, s32[256]{0:T(256)S(1)}, u32[]{:S(2)}, u32[]{:S(2)}) collective-permute-start(s32[256]{0:T(256)S(1)} %collective-permute-done.2), channel_id=1, source_target_pairs={{0,8},{8,16},{16,24},{24,32},{32,40},{40,48},{48,56},{56,64},{64,7... | collective-permute-start | bytes 3080 | tf_op jit(solution)/shard_map/ppermute | solution.py:21
  17.3 10.6 %copy-start.4 = (bf16[256,384]{0,1:T(8,128)(2,1)}, bf16[256,384]{0,1:T(8,128)(2,1)S(1)}, u32[]{:S(2)}) copy-start(bf16[256,384]{0,1:T(8,128)(2,1)S(1)} %copy.85) | copy-start | bytes 589828
  17.5 52.0 %copy-start.6 = (bf16[256,384]{0,1:T(8,128)(2,1)}, bf16[256,384]{0,1:T(8,128)(2,1)S(1)}, u32[]{:S(2)}) copy-start(bf16[256,384]{0,1:T(8,128)(2,1)S(1)} %copy.90) | copy-start | bytes 589828
  17.5 10.1 %collective-permute-start.6 = (s32[256]{0:T(256)S(1)}, s32[256]{0:T(256)S(1)}, u32[]{:S(2)}, u32[]{:S(2)}) collective-permute-start(s32[256]{0:T(256)S(1)} %collective-permute-done.4), channel_id=1, source_target_pairs={{0,8},{8,16},{16,24},{24,32},{32,40},{40,48},{48,56},{56,64},{64,7... | collective-permute-start | bytes 3080 | tf_op jit(solution)/shard_map/ppermute | solution.py:21
  21.8 5.6 %copy-start.38 = (bf16[256,384]{1,0:T(8,128)(2,1)S(1)}, bf16[256,384]{1,0:T(8,128)(2,1)}, u32[]{:S(2)}) copy-start(bf16[256,384]{1,0:T(8,128)(2,1)} %param.6) | copy-start | bytes 589828
  21.9 11.3 %collective-permute-start.1 = (bf16[2,256,384]{1,2,0:T(8,128)(2,1)S(1)}, bf16[2,256,384]{1,2,0:T(8,128)(2,1)S(1)}, u32[]{:S(2)}, u32[]{:S(2)}) collective-permute-start(bf16[2,256,384]{1,2,0:T(8,128)(2,1)S(1)} %pad_maximum_fusion), channel_id=1, source_target_pairs={{0,8},{8,16},{16,24},{24,32},{32,40},{40,48},{48,56},{56,64},{64,7... | collective-permute-start | bytes 1179656 | tf_op jit(solution)/shard_map/ppermute | solution.py:21
  27.9 41.9 %copy-start.14 = (pred[256,256]{0,1:T(8,128)(4,1)}, pred[256,256]{0,1:T(8,128)(4,1)S(1)}, u32[]{:S(2)}) copy-start(pred[256,256]{0,1:T(8,128)(4,1)S(1)} %get-tuple-element.33) | copy-start | bytes 196612
  27.9 42.2 %copy-start.12 = (pred[256,256]{0,1:T(8,128)(4,1)}, pred[256,256]{0,1:T(8,128)(4,1)S(1)}, u32[]{:S(2)}) copy-start(pred[256,256]{0,1:T(8,128)(4,1)S(1)} %get-tuple-element.34) | copy-start | bytes 196612
  27.9 42.5 %copy-start.10 = (pred[256,256]{0,1:T(8,128)(4,1)}, pred[256,256]{0,1:T(8,128)(4,1)S(1)}, u32[]{:S(2)}) copy-start(pred[256,256]{0,1:T(8,128)(4,1)S(1)} %get-tuple-element.35) | copy-start | bytes 196612
  27.9 42.9 %copy-start.8 = (pred[256,256]{0,1:T(8,128)(4,1)}, pred[256,256]{0,1:T(8,128)(4,1)S(1)}, u32[]{:S(2)}) copy-start(pred[256,256]{0,1:T(8,128)(4,1)S(1)} %get-tuple-element.36) | copy-start | bytes 196612
  33.2 10.6 %collective-permute-start.3 = (bf16[2,256,384]{1,2,0:T(8,128)(2,1)S(1)}, bf16[2,256,384]{1,2,0:T(8,128)(2,1)S(1)}, u32[]{:S(2)}, u32[]{:S(2)}) collective-permute-start(bf16[2,256,384]{1,2,0:T(8,128)(2,1)S(1)} %collective-permute-done.1), channel_id=1, source_target_pairs={{0,8},{8,16},{16,24},{24,32},{32,40},{40,48},{48,56},{56,64},{64,7... | collective-permute-start | bytes 1179656 | tf_op jit(solution)/shard_map/ppermute | solution.py:21
  38.4 31.4 %copy-start.18 = (bf16[1,256,384]{1,2,0:T(8,128)(2,1)}, bf16[1,256,384]{1,2,0:T(8,128)(2,1)S(1)}, u32[]{:S(2)}) copy-start(bf16[1,256,384]{1,2,0:T(8,128)(2,1)S(1)} %get-tuple-element.31) | copy-start | bytes 589828
  43.8 14.0 %collective-permute-start.5 = (bf16[2,256,384]{1,2,0:T(8,128)(2,1)S(1)}, bf16[2,256,384]{1,2,0:T(8,128)(2,1)S(1)}, u32[]{:S(2)}, u32[]{:S(2)}) collective-permute-start(bf16[2,256,384]{1,2,0:T(8,128)(2,1)S(1)} %collective-permute-done.3), channel_id=1, source_target_pairs={{0,8},{8,16},{16,24},{24,32},{32,40},{40,48},{48,56},{56,64},{64,7... | collective-permute-start | bytes 1179656 | tf_op jit(solution)/shard_map/ppermute | solution.py:21
  50.6 19.5 %copy-start.20 = (bf16[1,256,384]{1,2,0:T(8,128)(2,1)}, bf16[1,256,384]{1,2,0:T(8,128)(2,1)S(1)}, u32[]{:S(2)}) copy-start(bf16[1,256,384]{1,2,0:T(8,128)(2,1)S(1)} %get-tuple-element.29) | copy-start | bytes 589828
  57.9 10.3 %collective-permute-start.7 = (bf16[2,256,384]{1,2,0:T(8,128)(2,1)S(1)}, bf16[2,256,384]{1,2,0:T(8,128)(2,1)S(1)}, u32[]{:S(2)}, u32[]{:S(2)}) collective-permute-start(bf16[2,256,384]{1,2,0:T(8,128)(2,1)S(1)} %collective-permute-done.5), channel_id=1, source_target_pairs={{0,8},{8,16},{16,24},{24,32},{32,40},{40,48},{48,56},{56,64},{64,7... | collective-permute-start | bytes 1179656 | tf_op jit(solution)/shard_map/ppermute | solution.py:21
  62.9 7.5 %copy-start.22 = (bf16[1,256,384]{1,2,0:T(8,128)(2,1)}, bf16[1,256,384]{1,2,0:T(8,128)(2,1)S(1)}, u32[]{:S(2)}) copy-start(bf16[1,256,384]{1,2,0:T(8,128)(2,1)S(1)} %get-tuple-element.27) | copy-start | bytes 589828
  68.1 2.6 copy-start.24
  68.8 2.0 copy-start
  81.8 2.0 copy-start.36
  81.8 2.0 copy-start.39
  101.2 1.1 copy-start.15
  102.3 1.0 copy-start.19
  103.4 1.1 copy-start.13
  103.4 1.1 copy-start.21
  105.6 1.0 copy-start.11
  105.6 1.0 copy-start.23
  107.0 1.1 copy-start.1
  107.0 1.1 copy-start.9
  107.0 1.2 copy-start.25
  108.5 0.9 copy-start.7
  109.7 0.9 copy-start.32
  110.7 0.9 copy-start.33
  111.6 0.9 copy-start.34
  112.7 0.9 copy-start.5
  113.6 1.0 copy-start.3
  114.6 0.9 copy-start.27
  115.5 1.0 copy-start.2
  116.5 0.9 copy-start.29
  117.7 1.0 copy-start.31
  118.9 0.9 copy-start.35
  121.3 227.5 %collective-permute-start.8 = (bf16[2,256,384]{2,1,0:T(8,128)(2,1)}, bf16[2,256,384]{2,1,0:T(8,128)(2,1)S(1)}, u32[]{:S(2)}, u32[]{:S(2)}) collective-permute-start(bf16[2,256,384]{2,1,0:T(8,128)(2,1)} %pad_maximum_fusion.2), channel_id=1, source_target_pairs={{8,0},{16,8},{24,16},{32,24},{40,32},{48,40},{56,48},{64,56},{72,6... | collective-permute-start | bytes 1179656 | tf_op jit(solution)/shard_map/ppermute | solution.py:21
  123.4 225.4 %collective-permute-start.9 = (bf16[2,256,384]{2,1,0:T(8,128)(2,1)}, bf16[2,256,384]{2,1,0:T(8,128)(2,1)S(1)}, u32[]{:S(2)}, u32[]{:S(2)}) collective-permute-start(bf16[2,256,384]{2,1,0:T(8,128)(2,1)} %pad_maximum_fusion.3), channel_id=1, source_target_pairs={{16,0},{24,8},{32,16},{40,24},{48,32},{56,40},{64,48},{72,56},{80,... | collective-permute-start | bytes 1179656 | tf_op jit(solution)/shard_map/ppermute | solution.py:21
  125.5 3.5 %copy-start.17 = (bf16[1,256,384]{1,2,0:T(8,128)(2,1)S(1)}, bf16[1,256,384]{1,2,0:T(8,128)(2,1)}, u32[]{:S(2)}) copy-start(bf16[1,256,384]{1,2,0:T(8,128)(2,1)} %copy-done.16) | copy-start | bytes 589828
  125.5 223.3 %collective-permute-start.11 = (bf16[2,256,384]{2,1,0:T(8,128)(2,1)}, bf16[2,256,384]{2,1,0:T(8,128)(2,1)S(1)}, u32[]{:S(2)}, u32[]{:S(2)}) collective-permute-start(bf16[2,256,384]{2,1,0:T(8,128)(2,1)} %pad_maximum_fusion.5), channel_id=1, source_target_pairs={{32,0},{40,8},{48,16},{56,24},{64,32},{72,40},{80,48},{88,56},{96,... | collective-permute-start | bytes 1179656 | tf_op jit(solution)/shard_map/ppermute | solution.py:21
  127.7 221.1 %collective-permute-start.10 = (bf16[2,256,384]{2,1,0:T(8,128)(2,1)}, bf16[2,256,384]{2,1,0:T(8,128)(2,1)}, u32[]{:S(2)}, u32[]{:S(2)}) collective-permute-start(bf16[2,256,384]{2,1,0:T(8,128)(2,1)} %pad_maximum_fusion.4), channel_id=1, source_target_pairs={{24,0},{32,8},{40,16},{48,24},{56,32},{64,40},{72,48},{80,56},{88,... | collective-permute-start | bytes 1179656 | tf_op jit(solution)/shard_map/ppermute | solution.py:21
  (5 other events, 3.4 us)
where the time goes:
time: 352 us; the launch traced here: 351 us
  blocking collectives  239 us (68%)
  starting transfers between devices  44.2 us (13%)
  waiting for transfers between devices  23.4 us (7%)
  local copies, waits for them, and re-layouts  16.8 us (5%)
  matrix products  14 us (4%)
  other arithmetic  11.7 us (3%)
    psum x1, blocking collectives, body(): lax.psum(jnp.sum(grad_rows * flat_att * rms_inv[:, None], axis=0), 'tm')  217 us
    ppermute x12, starting transfers between devices, passed_along(): return lax.ppermute(x, axis, pairs)  44.2 us
    ppermute x12, waiting for transfers between devices, passed_along(): return lax.ppermute(x, axis, pairs)  23.4 us
    psum x2, blocking collectives, body(): lax.psum((jnp.sum(flat_att * flat_att, axis=1), jnp.sum(scaled * flat_att...  22 us
    unnamed x86, local copies, waits for them, and re-layouts  11.2 us
  transfers between devices with their start and end apart: 12, of which 6 were waited for; matrix products, arithmetic and copies ran while one was open for 2% of the time, Pallas kernels for 0%

commit v1 on v0

--- a/solution.py
+++ b/solution.py
@@ -173,7 +173,9 @@
     grad_att = (
         rms_inv[:, None] * (scaled - flat_att * (rms_inv * rms_inv * cross_sum / features)[:, None])
     ).astype(jnp.bfloat16)
-    grad_gain = lax.psum(jnp.sum(grad_rows * flat_att * rms_inv[:, None], axis=0), "tm")
+    value = jnp.sum(grad_rows * flat_att * rms_inv[:, None], axis=0)
+    parts = lax.all_gather(value, "tm", axis=0, tiled=False)
+    grad_gain = parts.sum(axis=0)
     grad_heads = grad_att.reshape(layout)
     row_delta = jnp.sum(attended.astype(jnp.float32) * grad_heads.astype(jnp.float32), axis=2).T
     zero_heads = jnp.zeros(layout, jnp.float32)

time: 352 us -> 313 us (0.89)
  blocking collectives: 239 us -> 197 us
    psum x1 -> x0, blocking collectives: 217 us -> none  [body(): lax.psum(jnp.sum(grad_rows * flat_att * rms_inv[:, None], axis=0), 'tm')]
    all_gather x0 -> x1, blocking collectives: none -> 175 us  [body(): parts = lax.all_gather(value, 'tm', axis=0, tiled=False)]
    unnamed x86 -> x95, local copies, waits for them, and re-layouts: 11.2 us -> 9.38 us
  transfers between devices with their start and end apart: 12 -> 12, of which waited for: 6 -> 6; matrix products, arithmetic and copies ran while one was open for 2% -> 3% of each run, Pallas kernels for 0% -> 0%
where the time goes in v1:
time: 313 us; the launch traced here: 310 us
  blocking collectives  197 us (63%)
  starting transfers between devices  44.4 us (14%)
  waiting for transfers between devices  23.4 us (7%)
  local copies, waits for them, and re-layouts  16.9 us (5%)
  matrix products  14.7 us (5%)
  other arithmetic  12.3 us (4%)
    all_gather x1, blocking collectives, body(): parts = lax.all_gather(value, 'tm', axis=0, tiled=False)  175 us
    ppermute x12, starting transfers between devices, passed_along(): return lax.ppermute(x, axis, pairs)  44.4 us
    ppermute x12, waiting for transfers between devices, passed_along(): return lax.ppermute(x, axis, pairs)  23.4 us
    psum x2, blocking collectives, body(): lax.psum((jnp.sum(flat_att * flat_att, axis=1), jnp.sum(scaled * flat_att...  22 us
    unnamed x95, local copies, waits for them, and re-layouts  9.38 us
  transfers between devices with their start and end apart: 12, of which 6 were waited for; matrix products, arithmetic and copies ran while one was open for 3% of the time, Pallas kernels for 0%

profile of v1, /device:TPU:6, one launch (start us, length us, event | category | flops | bytes accessed | tf_op | source)
XLA Modules:
  0.0 310.1 jit_solution(3753476366251063156)
XLA Ops:
  1.4 3.9 %collective-permute-start = (s32[256]{0:T(256)S(1)}, s32[256]{0:T(256)S(1)}, u32[]{:S(2)}, u32[]{:S(2)}) collective-permute-start(s32[256]{0:T(256)S(1)} %broadcast_bitcast_fusion), channel_id=1, source_target_pairs={{0,8},{8,16},{16,24},{24,32},{32,40},{40,48},{48,56},{56,64},{64,7... | collective-permute-start | bytes 3080 | tf_op jit(solution)/shard_map/ppermute | solution.py:21
  5.3 1.3 collective-permute-done
  6.6 4.2 %collective-permute-start.2 = (s32[256]{0:T(256)S(1)}, s32[256]{0:T(256)S(1)}, u32[]{:S(2)}, u32[]{:S(2)}) collective-permute-start(s32[256]{0:T(256)S(1)} %collective-permute-done), channel_id=1, source_target_pairs={{0,8},{8,16},{16,24},{24,32},{32,40},{40,48},{48,56},{56,64},{64,7... | collective-permute-start | bytes 3080 | tf_op jit(solution)/shard_map/ppermute | solution.py:21
  10.8 1.3 collective-permute-done.2
  12.0 4.2 %collective-permute-start.4 = (s32[256]{0:T(256)S(1)}, s32[256]{0:T(256)S(1)}, u32[]{:S(2)}, u32[]{:S(2)}) collective-permute-start(s32[256]{0:T(256)S(1)} %collective-permute-done.2), channel_id=1, source_target_pairs={{0,8},{8,16},{16,24},{24,32},{32,40},{40,48},{48,56},{56,64},{64,7... | collective-permute-start | bytes 3080 | tf_op jit(solution)/shard_map/ppermute | solution.py:21
  16.2 1.1 copy.152
  17.5 4.3 %collective-permute-start.6 = (s32[256]{0:T(256)S(1)}, s32[256]{0:T(256)S(1)}, u32[]{:S(2)}, u32[]{:S(2)}) collective-permute-start(s32[256]{0:T(256)S(1)} %collective-permute-done.4), channel_id=1, source_target_pairs={{0,8},{8,16},{16,24},{24,32},{32,40},{40,48},{48,56},{56,64},{64,7... | collective-permute-start | bytes 3080 | tf_op jit(solution)/shard_map/ppermute | solution.py:21
  21.9 5.5 %collective-permute-start.1 = (bf16[2,256,384]{1,2,0:T(8,128)(2,1)S(1)}, bf16[2,256,384]{1,2,0:T(8,128)(2,1)S(1)}, u32[]{:S(2)}, u32[]{:S(2)}) collective-permute-start(bf16[2,256,384]{1,2,0:T(8,128)(2,1)S(1)} %pad_maximum_fusion), channel_id=1, source_target_pairs={{0,8},{8,16},{16,24},{24,32},{32,40},{40,48},{48,56},{56,64},{64,7... | collective-permute-start | bytes 1179656 | tf_op jit(solution)/shard_map/ppermute | solution.py:21
  28.4 4.8 %collective-permute-done.1 = bf16[2,256,384]{1,2,0:T(8,128)(2,1)S(1)} collective-permute-done((bf16[2,256,384]{1,2,0:T(8,128)(2,1)S(1)}, bf16[2,256,384]{1,2,0:T(8,128)(2,1)S(1)}, u32[]{:S(2)}, u32[]{:S(2)}) %collective-permute-start.1) | collective-permute-done | bytes 393248 | tf_op jit(solution)/shard_map/ppermute | solution.py:21
  33.2 5.1 %collective-permute-start.3 = (bf16[2,256,384]{1,2,0:T(8,128)(2,1)S(1)}, bf16[2,256,384]{1,2,0:T(8,128)(2,1)S(1)}, u32[]{:S(2)}, u32[]{:S(2)}) collective-permute-start(bf16[2,256,384]{1,2,0:T(8,128)(2,1)S(1)} %collective-permute-done.1), channel_id=1, source_target_pairs={{0,8},{8,16},{16,24},{24,32},{32,40},{40,48},{48,56},{56,64},{64,7... | collective-permute-start | bytes 1179656 | tf_op jit(solution)/shard_map/ppermute | solution.py:21
  39.0 4.8 %collective-permute-done.3 = bf16[2,256,384]{1,2,0:T(8,128)(2,1)S(1)} collective-permute-done((bf16[2,256,384]{1,2,0:T(8,128)(2,1)S(1)}, bf16[2,256,384]{1,2,0:T(8,128)(2,1)S(1)}, u32[]{:S(2)}, u32[]{:S(2)}) %collective-permute-start.3) | collective-permute-done | bytes 393248 | tf_op jit(solution)/shard_map/ppermute | solution.py:21
  43.8 6.7 %collective-permute-start.5 = (bf16[2,256,384]{1,2,0:T(8,128)(2,1)S(1)}, bf16[2,256,384]{1,2,0:T(8,128)(2,1)S(1)}, u32[]{:S(2)}, u32[]{:S(2)}) collective-permute-start(bf16[2,256,384]{1,2,0:T(8,128)(2,1)S(1)} %collective-permute-done.3), channel_id=1, source_target_pairs={{0,8},{8,16},{16,24},{24,32},{32,40},{40,48},{48,56},{56,64},{64,7... | collective-permute-start | bytes 1179656 | tf_op jit(solution)/shard_map/ppermute | solution.py:21
  51.2 6.6 %collective-permute-done.5 = bf16[2,256,384]{1,2,0:T(8,128)(2,1)S(1)} collective-permute-done((bf16[2,256,384]{1,2,0:T(8,128)(2,1)S(1)}, bf16[2,256,384]{1,2,0:T(8,128)(2,1)S(1)}, u32[]{:S(2)}, u32[]{:S(2)}) %collective-permute-start.5) | collective-permute-done | bytes 393248 | tf_op jit(solution)/shard_map/ppermute | solution.py:21
  57.9 5.0 %collective-permute-start.7 = (bf16[2,256,384]{1,2,0:T(8,128)(2,1)S(1)}, bf16[2,256,384]{1,2,0:T(8,128)(2,1)S(1)}, u32[]{:S(2)}, u32[]{:S(2)}) collective-permute-start(bf16[2,256,384]{1,2,0:T(8,128)(2,1)S(1)} %collective-permute-done.5), channel_id=1, source_target_pairs={{0,8},{8,16},{16,24},{24,32},{32,40},{40,48},{48,56},{56,64},{64,7... | collective-permute-start | bytes 1179656 | tf_op jit(solution)/shard_map/ppermute | solution.py:21
  63.6 4.5 %collective-permute-done.7 = bf16[2,256,384]{1,2,0:T(8,128)(2,1)S(1)} collective-permute-done((bf16[2,256,384]{1,2,0:T(8,128)(2,1)S(1)}, bf16[2,256,384]{1,2,0:T(8,128)(2,1)S(1)}, u32[]{:S(2)}, u32[]{:S(2)}) %collective-permute-start.7) | collective-permute-done | bytes 393248 | tf_op jit(solution)/shard_map/ppermute | solution.py:21
  70.8 1.1 multiply_reduce_fusion.1
  71.8 10.0 %psum.14 = f32[256]{0:T(256)S(1)} all-reduce(f32[256]{0:T(256)S(1)} %get-tuple-element.53), channel_id=1, replica_groups=mesh['tm'=64,'head'=8] {'head'}, use_global_device_ids=true, to_apply=%region_11.12 | all-reduce | flops 256 | bytes 2048 | tf_op jit(solution)/shard_map/psum | solution.py:168
  81.8 2.0 copy.172
  83.8 1.7 fusion.47
  85.5 12.0 %psum.15 = f32[256]{0:T(256)} all-reduce(f32[256]{0:T(256)} %get-tuple-element.21), channel_id=1, replica_groups=mesh['tm'=64,'head'=8] {'head'}, use_global_device_ids=true, to_apply=%region_13.14 | all-reduce | flops 256 | bytes 2048 | tf_op jit(solution)/shard_map/psum | solution.py:168
  98.3 1.9 fusion.45
  100.2 1.1 copy.175
  101.2 1.1 multiply_reduce_fusion
  102.4 1.0 convolution_convert_fusion.3
  103.4 1.1 fusion.11
  104.5 1.1 fusion.12
  105.6 1.0 convolution_convert_fusion.2
  107.0 1.0 convolution_convert_fusion.1
  109.8 1.0 convolution_convert_fusion.4
  110.7 0.8 copy.203
  111.7 0.8 copy.207
  112.8 0.8 copy.215
  113.9 0.8 copy-done.3
  114.7 1.0 fusion.30
  115.9 0.8 copy-done.2
  120.7 0.8 copy-done.38
  121.5 0.8 pad_maximum_fusion.2
  122.2 1.4 collective-permute-start.8
  123.7 0.8 pad_maximum_fusion.3
  124.5 1.3 collective-permute-start.9
  125.8 0.8 pad_maximum_fusion.5
  126.6 1.4 collective-permute-start.11
  128.0 0.8 pad_maximum_fusion.4
  128.8 1.4 collective-permute-start.10
  131.1 0.8 copy.217
  132.4 174.9 %all-gather.1 = f32[64,1,384]{2,1,0:T(1,128)S(1)} all-gather(f32[1,1,384]{2,1,0:T(1,128)S(1)} %reshape.258), channel_id=2, replica_groups=mesh['tm'=64,'head'=8] {'tm'}, dimensions={0}, use_global_device_ids=true | all-gather | bytes 99840 | tf_op jit(solution)/shard_map/all_gather | solution.py:177
  308.1 1.2 add_convert_fusion
  309.3 0.8 slice_bitcast_fusion
  (142 shorter events, 16.1 us)
Async XLA Ops:
  1.4 15.9 %copy-start.41 = (bf16[256,384]{1,0:T(8,128)(2,1)S(1)}, bf16[256,384]{1,0:T(8,128)(2,1)}, u32[]{:S(2)}) copy-start(bf16[256,384]{1,0:T(8,128)(2,1)} %param.8) | copy-start | bytes 589828
  1.4 5.2 %collective-permute-start = (s32[256]{0:T(256)S(1)}, s32[256]{0:T(256)S(1)}, u32[]{:S(2)}, u32[]{:S(2)}) collective-permute-start(s32[256]{0:T(256)S(1)} %broadcast_bitcast_fusion), channel_id=1, source_target_pairs={{0,8},{8,16},{16,24},{24,32},{32,40},{40,48},{48,56},{56,64},{64,7... | collective-permute-start | bytes 3080 | tf_op jit(solution)/shard_map/ppermute | solution.py:21
  6.6 5.5 %collective-permute-start.2 = (s32[256]{0:T(256)S(1)}, s32[256]{0:T(256)S(1)}, u32[]{:S(2)}, u32[]{:S(2)}) collective-permute-start(s32[256]{0:T(256)S(1)} %collective-permute-done), channel_id=1, source_target_pairs={{0,8},{8,16},{16,24},{24,32},{32,40},{40,48},{48,56},{56,64},{64,7... | collective-permute-start | bytes 3080 | tf_op jit(solution)/shard_map/ppermute | solution.py:21
  12.0 5.5 %collective-permute-start.4 = (s32[256]{0:T(256)S(1)}, s32[256]{0:T(256)S(1)}, u32[]{:S(2)}, u32[]{:S(2)}) collective-permute-start(s32[256]{0:T(256)S(1)} %collective-permute-done.2), channel_id=1, source_target_pairs={{0,8},{8,16},{16,24},{24,32},{32,40},{40,48},{48,56},{56,64},{64,7... | collective-permute-start | bytes 3080 | tf_op jit(solution)/shard_map/ppermute | solution.py:21
  17.3 10.6 %copy-start.4 = (bf16[256,384]{0,1:T(8,128)(2,1)}, bf16[256,384]{0,1:T(8,128)(2,1)S(1)}, u32[]{:S(2)}) copy-start(bf16[256,384]{0,1:T(8,128)(2,1)S(1)} %copy.152) | copy-start | bytes 589828
  17.5 52.0 %copy-start.6 = (bf16[256,384]{0,1:T(8,128)(2,1)}, bf16[256,384]{0,1:T(8,128)(2,1)S(1)}, u32[]{:S(2)}) copy-start(bf16[256,384]{0,1:T(8,128)(2,1)S(1)} %copy.157) | copy-start | bytes 589828
  17.5 10.1 %collective-permute-start.6 = (s32[256]{0:T(256)S(1)}, s32[256]{0:T(256)S(1)}, u32[]{:S(2)}, u32[]{:S(2)}) collective-permute-start(s32[256]{0:T(256)S(1)} %collective-permute-done.4), channel_id=1, source_target_pairs={{0,8},{8,16},{16,24},{24,32},{32,40},{40,48},{48,56},{56,64},{64,7... | collective-permute-start | bytes 3080 | tf_op jit(solution)/shard_map/ppermute | solution.py:21
  21.8 5.6 %copy-start.42 = (bf16[256,384]{1,0:T(8,128)(2,1)S(1)}, bf16[256,384]{1,0:T(8,128)(2,1)}, u32[]{:S(2)}) copy-start(bf16[256,384]{1,0:T(8,128)(2,1)} %param.6) | copy-start | bytes 589828
  21.9 11.3 %collective-permute-start.1 = (bf16[2,256,384]{1,2,0:T(8,128)(2,1)S(1)}, bf16[2,256,384]{1,2,0:T(8,128)(2,1)S(1)}, u32[]{:S(2)}, u32[]{:S(2)}) collective-permute-start(bf16[2,256,384]{1,2,0:T(8,128)(2,1)S(1)} %pad_maximum_fusion), channel_id=1, source_target_pairs={{0,8},{8,16},{16,24},{24,32},{32,40},{40,48},{48,56},{56,64},{64,7... | collective-permute-start | bytes 1179656 | tf_op jit(solution)/shard_map/ppermute | solution.py:21
  27.9 41.9 %copy-start.14 = (pred[256,256]{0,1:T(8,128)(4,1)}, pred[256,256]{0,1:T(8,128)(4,1)S(1)}, u32[]{:S(2)}) copy-start(pred[256,256]{0,1:T(8,128)(4,1)S(1)} %get-tuple-element.38) | copy-start | bytes 196612
  27.9 42.2 %copy-start.12 = (pred[256,256]{0,1:T(8,128)(4,1)}, pred[256,256]{0,1:T(8,128)(4,1)S(1)}, u32[]{:S(2)}) copy-start(pred[256,256]{0,1:T(8,128)(4,1)S(1)} %get-tuple-element.39) | copy-start | bytes 196612
  27.9 42.5 %copy-start.10 = (pred[256,256]{0,1:T(8,128)(4,1)}, pred[256,256]{0,1:T(8,128)(4,1)S(1)}, u32[]{:S(2)}) copy-start(pred[256,256]{0,1:T(8,128)(4,1)S(1)} %get-tuple-element.40) | copy-start | bytes 196612
  27.9 42.8 %copy-start.8 = (pred[256,256]{0,1:T(8,128)(4,1)}, pred[256,256]{0,1:T(8,128)(4,1)S(1)}, u32[]{:S(2)}) copy-start(pred[256,256]{0,1:T(8,128)(4,1)S(1)} %get-tuple-element.41) | copy-start | bytes 196612
  33.2 10.6 %collective-permute-start.3 = (bf16[2,256,384]{1,2,0:T(8,128)(2,1)S(1)}, bf16[2,256,384]{1,2,0:T(8,128)(2,1)S(1)}, u32[]{:S(2)}, u32[]{:S(2)}) collective-permute-start(bf16[2,256,384]{1,2,0:T(8,128)(2,1)S(1)} %collective-permute-done.1), channel_id=1, source_target_pairs={{0,8},{8,16},{16,24},{24,32},{32,40},{40,48},{48,56},{56,64},{64,7... | collective-permute-start | bytes 1179656 | tf_op jit(solution)/shard_map/ppermute | solution.py:21
  38.4 31.4 %copy-start.18 = (bf16[1,256,384]{1,2,0:T(8,128)(2,1)}, bf16[1,256,384]{1,2,0:T(8,128)(2,1)S(1)}, u32[]{:S(2)}) copy-start(bf16[1,256,384]{1,2,0:T(8,128)(2,1)S(1)} %get-tuple-element.36) | copy-start | bytes 589828
  43.8 14.0 %collective-permute-start.5 = (bf16[2,256,384]{1,2,0:T(8,128)(2,1)S(1)}, bf16[2,256,384]{1,2,0:T(8,128)(2,1)S(1)}, u32[]{:S(2)}, u32[]{:S(2)}) collective-permute-start(bf16[2,256,384]{1,2,0:T(8,128)(2,1)S(1)} %collective-permute-done.3), channel_id=1, source_target_pairs={{0,8},{8,16},{16,24},{24,32},{32,40},{40,48},{48,56},{56,64},{64,7... | collective-permute-start | bytes 1179656 | tf_op jit(solution)/shard_map/ppermute | solution.py:21
  50.6 19.5 %copy-start.20 = (bf16[1,256,384]{1,2,0:T(8,128)(2,1)}, bf16[1,256,384]{1,2,0:T(8,128)(2,1)S(1)}, u32[]{:S(2)}) copy-start(bf16[1,256,384]{1,2,0:T(8,128)(2,1)S(1)} %get-tuple-element.34) | copy-start | bytes 589828
  57.9 10.3 %collective-permute-start.7 = (bf16[2,256,384]{1,2,0:T(8,128)(2,1)S(1)}, bf16[2,256,384]{1,2,0:T(8,128)(2,1)S(1)}, u32[]{:S(2)}, u32[]{:S(2)}) collective-permute-start(bf16[2,256,384]{1,2,0:T(8,128)(2,1)S(1)} %collective-permute-done.5), channel_id=1, source_target_pairs={{0,8},{8,16},{16,24},{24,32},{32,40},{40,48},{48,56},{56,64},{64,7... | collective-permute-start | bytes 1179656 | tf_op jit(solution)/shard_map/ppermute | solution.py:21
  62.9 7.5 %copy-start.22 = (bf16[1,256,384]{1,2,0:T(8,128)(2,1)}, bf16[1,256,384]{1,2,0:T(8,128)(2,1)S(1)}, u32[]{:S(2)}) copy-start(bf16[1,256,384]{1,2,0:T(8,128)(2,1)S(1)} %get-tuple-element.32) | copy-start | bytes 589828
  68.1 2.6 copy-start.24
  68.8 2.0 copy-start
  81.8 2.0 copy-start.40
  81.8 2.0 copy-start.43
  101.2 1.1 copy-start.15
  102.3 1.0 copy-start.19
  103.4 1.1 copy-start.13
  103.4 1.1 copy-start.21
  105.6 1.0 copy-start.11
  105.6 1.0 copy-start.23
  107.0 1.1 copy-start.1
  107.0 1.1 copy-start.9
  107.0 1.2 copy-start.25
  108.5 0.9 copy-start.7
  109.8 1.0 copy-start.33
  112.8 0.9 copy-start.5
  113.7 1.0 copy-start.3
  114.7 1.0 copy-start.27
  115.7 1.0 copy-start.2
  117.8 0.9 copy-start.31
  119.6 0.9 copy-start.39
  121.5 2.2 copy-start.37
  122.2 3.5 %copy-start.36 = (bf16[1,256,384]{2,1,0:T(8,128)(2,1)S(1)}, bf16[1,256,384]{2,1,0:T(8,128)(2,1)}, u32[]{:S(2)}) copy-start(bf16[1,256,384]{2,1,0:T(8,128)(2,1)} %copy.215) | copy-start | bytes 589828
  122.2 185.8 %collective-permute-start.8 = (bf16[2,256,384]{2,1,0:T(8,128)(2,1)}, bf16[2,256,384]{2,1,0:T(8,128)(2,1)S(1)}, u32[]{:S(2)}, u32[]{:S(2)}) collective-permute-start(bf16[2,256,384]{2,1,0:T(8,128)(2,1)} %pad_maximum_fusion.2), channel_id=1, source_target_pairs={{8,0},{16,8},{24,16},{32,24},{40,32},{48,40},{56,48},{64,56},{72,6... | collective-permute-start | bytes 1179656 | tf_op jit(solution)/shard_map/ppermute | solution.py:21
  124.5 183.6 %collective-permute-start.9 = (bf16[2,256,384]{2,1,0:T(8,128)(2,1)}, bf16[2,256,384]{2,1,0:T(8,128)(2,1)S(1)}, u32[]{:S(2)}, u32[]{:S(2)}) collective-permute-start(bf16[2,256,384]{2,1,0:T(8,128)(2,1)} %pad_maximum_fusion.3), channel_id=1, source_target_pairs={{16,0},{24,8},{32,16},{40,24},{48,32},{56,40},{64,48},{72,56},{80,... | collective-permute-start | bytes 1179656 | tf_op jit(solution)/shard_map/ppermute | solution.py:21
  126.6 3.7 %copy-start.17 = (bf16[1,256,384]{1,2,0:T(8,128)(2,1)S(1)}, bf16[1,256,384]{1,2,0:T(8,128)(2,1)}, u32[]{:S(2)}) copy-start(bf16[1,256,384]{1,2,0:T(8,128)(2,1)} %copy-done.16) | copy-start | bytes 589828
  126.6 181.5 %collective-permute-start.11 = (bf16[2,256,384]{2,1,0:T(8,128)(2,1)}, bf16[2,256,384]{2,1,0:T(8,128)(2,1)S(1)}, u32[]{:S(2)}, u32[]{:S(2)}) collective-permute-start(bf16[2,256,384]{2,1,0:T(8,128)(2,1)} %pad_maximum_fusion.5), channel_id=1, source_target_pairs={{32,0},{40,8},{48,16},{56,24},{64,32},{72,40},{80,48},{88,56},{96,... | collective-permute-start | bytes 1179656 | tf_op jit(solution)/shard_map/ppermute | solution.py:21
  128.8 2.1 copy-start.32
  128.8 179.3 %collective-permute-start.10 = (bf16[2,256,384]{2,1,0:T(8,128)(2,1)}, bf16[2,256,384]{2,1,0:T(8,128)(2,1)}, u32[]{:S(2)}, u32[]{:S(2)}) collective-permute-start(bf16[2,256,384]{2,1,0:T(8,128)(2,1)} %pad_maximum_fusion.4), channel_id=1, source_target_pairs={{24,0},{32,8},{40,16},{48,24},{56,32},{64,40},{72,48},{80,56},{88,... | collective-permute-start | bytes 1179656 | tf_op jit(solution)/shard_map/ppermute | solution.py:21
  (9 other events, 7.1 us)
